TPU v7x, 32 devices: a whole 2x2x4 slice. The times are simulated.
32 devices in a mesh: probe: 2 (over x), space: 16 (over z, y, core).
Axes of the slice: x: 2, y: 2, z: 4, core: 2. Of those that a mesh axis runs over, the one named last changes fastest.
Arguments:
- field_before: float32 [2, 64, 256, 256], P('probe', 'space'), may hold values from -6 to 6
- field_now: float32 [2, 64, 256, 256], P('probe', 'space'), may hold values from -6 to 6
- stiffness: float32 [64, 256, 256], P('space'), may hold values from 0.04 to 0.1
- buoyancy: float32 [64, 256, 256], P('space'), may hold values from 0.6 to 1.4
- perturbation: float32 [2, 64, 256, 256], P('probe', 'space'), may hold values from -0.25 to 0.25
Outputs:
- field_after: float32 [2, 64, 256, 256], P('probe', 'space')
All inputs are finite; a program needn't handle non-finite values.
Results may differ from a plain program's by a relative error of at most 0.00002.
Values sent between devices are 32-bit elements; how exact they have to be, the bound alone decides.
No kernel may reach another device: no remote copies, remote signals or barrier semaphores. Data moves between devices by JAX's collectives and lax.ppermute only.
A program may use at most 128 MiB of HBM per device.

v0:
```python
import jax
import jax.numpy as jnp
from jax import lax
from jax.sharding import PartitionSpec as P

STEPS = 2
second_coeffs = (8.0 / 5.0, -1.0 / 5.0, 8.0 / 315.0, -1.0 / 560.0)
first_coeffs = (4.0 / 5.0, -1.0 / 5.0, 4.0 / 105.0, -1.0 / 280.0)
centre_coeff = -205.0 / 72.0


def with_halo(block, sides, width):
    for axis, dim in sides:
        count = lax.axis_size(axis)
        forward = [(i, i + 1) for i in range(count - 1)]
        backward = [(target, source) for source, target in forward]
        low = lax.ppermute(
            lax.slice_in_dim(block, block.shape[dim] - width, None, axis=dim), axis, forward
        )
        high = lax.ppermute(lax.slice_in_dim(block, 0, width, axis=dim), axis, backward)
        block = jnp.concatenate([low, block, high], axis=dim)
    return block


def spread(block, axis, owner):
    block = jnp.where(lax.axis_index(axis) == owner, block, jnp.zeros_like(block))
    return lax.psum(block, axis)


def shifted(padded, direction, offset):
    window = [
        slice(4, padded.shape[0] - 4),
        slice(4, padded.shape[1] - 4),
        slice(4, padded.shape[2] - 4),
    ]
    window[direction] = slice(4 + offset, padded.shape[direction] - 4 + offset)
    return padded[tuple(window)]


def second_sum(padded):
    total = 3.0 * centre_coeff * shifted(padded, 0, 0)
    for direction in range(3):
        for reach in range(1, 5):
            total = total + second_coeffs[reach - 1] * (
                shifted(padded, direction, reach) + shifted(padded, direction, -reach)
            )
    return total


def first_parts(padded):
    parts = []
    for direction in range(3):
        total = jnp.zeros_like(shifted(padded, 0, 0))
        for reach in range(1, 5):
            total = total + first_coeffs[reach - 1] * (
                shifted(padded, direction, reach) - shifted(padded, direction, -reach)
            )
        parts.append(total)
    return parts


def pad_sides(extended):
    return jnp.pad(extended, ((0, 0), (4, 4), (4, 4)))


def divergence(padded, buoyancy, slope):
    grads = first_parts(padded)
    return (
        buoyancy * second_sum(padded)
        + slope[0] * grads[0]
        + slope[1] * grads[1]
        + slope[2] * grads[2]
    )


def on_device(field_before, field_now, stiffness, buoyancy, perturbation):
    rim = with_halo(buoyancy - 1.0, (("space", 0),), 4)
    slope = first_parts(pad_sides(rim))
    born_flag = (lax.axis_index("probe") > 0).astype(jnp.float32)
    source_scale = born_flag * perturbation[0]

    def operate(extended):
        return divergence(pad_sides(extended), buoyancy, slope)

    before = field_before[0]
    now = field_now[0]
    for step in range(STEPS):
        base = spread(now, "probe", 0)
        both = with_halo(jnp.stack([base, now]), (("space", 1),), 4)
        base_term = operate(both[0])
        own_term = operate(both[1])
        following = 2.0 * now - before + stiffness * own_term + source_scale * base_term
        before, now = (now, following)
    return now[None]


def solution(mesh):
    placed = (
        P("probe", "space", None, None),
        P("probe", "space", None, None),
        P("space", None, None),
        P("space", None, None),
        P("probe", "space", None, None),
    )
    return jax.shard_map(
        on_device,
        mesh=mesh,
        in_specs=placed,
        out_specs=P("probe", "space", None, None),
        check_vma=False,
    )
```

profile of v0, /device:TPU:9, one launch (start us, length us, event | category | flops | bytes accessed | tf_op | source)
XLA Modules:
  0.0 317.0 jit_solution(4905952962133589606)
XLA Ops:
  6.5 2.4 bitcast_select_fusion
  9.0 41.9 %all-reduce.8.cloned.1.call-done = f32[4,256,256]{2,1,0:T(8,128)} async-done(((f32[4,256,256]{2,1,0:T(8,128)}), f32[4,256,256]{2,1,0:T(8,128)}) %all-reduce.8.cloned.1.call-update) | async-done | bytes 1048592 | tf_op jit(solution)/shard_map/psum | solution.py:27
  50.9 3.0 pad_maximum_fusion.4
  53.9 3.6 %collective-permute-start.1 = (f32[2,4,256,256]{3,2,1,0:T(8,128)}, f32[2,4,256,256]{3,2,1,0:T(8,128)S(1)}, u32[]{:S(2)}, u32[]{:S(2)}) collective-permute-start(f32[2,4,256,256]{3,2,1,0:T(8,128)} %pad_maximum_fusion.4), channel_id=1, source_target_pairs={{0,1},{1,2},{2,3},{3,4},{4,5},{5,6},{6,7},{7,8},{8,9},{9,10},{10,1... | collective-permute-start | bytes 6291464 | tf_op jit(solution)/shard_map/ppermute | solution.py:17
  57.6 1.9 collective-permute-start
  59.5 1.1 broadcast_add_fusion
  60.6 3.8 %collective-permute-start.3 = (f32[4,256,256]{2,1,0:T(8,128)}, f32[4,256,256]{2,1,0:T(8,128)}, u32[]{:S(2)}, u32[]{:S(2)}) collective-permute-start(f32[4,256,256]{2,1,0:T(8,128)} %broadcast_add_fusion), channel_id=1, source_target_pairs={{0,1},{1,2},{2,3},{3,4},{4,5},{5,6},{6,7},{7,8},{8,9},{9,10},{10,1... | collective-permute-start | bytes 3145736 | tf_op jit(solution)/shard_map/ppermute | solution.py:17
  64.3 1.9 collective-permute-start.2
  66.3 59.5 %collective-permute-done.3 = f32[4,256,256]{2,1,0:T(8,128)} collective-permute-done((f32[4,256,256]{2,1,0:T(8,128)}, f32[4,256,256]{2,1,0:T(8,128)}, u32[]{:S(2)}, u32[]{:S(2)}) %collective-permute-start.3) | collective-permute-done | bytes 1048608 | tf_op jit(solution)/shard_map/ppermute | solution.py:17
  125.8 1.6 collective-permute-done.2
  127.4 5.4 %select_maximum_fusion = f32[12,264,264]{2,1,0:T(8,128)} fusion(f32[4,256,256]{2,1,0:T(8,128)} %collective-permute-done.2, f32[4,256,256]{2,1,0:T(8,128)} %broadcast_add_fusion, f32[4,256,256]{2,1,0:T(8,128)} %collective-permute-done.3), kind=kLoop, calls=%fused_computation.70 | loop fusion | flops 12545280 | bytes 6491136 | tf_op jit(solution)/shard_map/concatenate | solution.py:21
  132.8 2.7 pad_maximum_fusion
  135.5 3.2 %slice_bitcast_fusion.3 = (f32[12,256,256]{2,1,0:T(8,128)}, f32[12,256,256]{2,1,0:T(8,128)}) fusion(f32[2,12,256,256]{3,2,1,0:T(8,128)S(1)} %pad_maximum_fusion), kind=kLoop, calls=%fused_computation.82 | loop fusion | bytes 12582912 | tf_op jit(solution)/shard_map/squeeze | solution.py:91
  138.8 5.0 %pad_maximum_fusion.2 = (f32[2,8,256,256]{3,2,1,0:T(8,128)}, f32[2,8,256,256]{3,2,1,0:T(8,128)}) fusion(f32[2,4,256,256]{3,2,1,0:T(8,128)} %collective-permute-done, f32[1,4,256,256]{3,2,1,0:T(8,128)S(1)} %copy-done, f32[1,4,256,256]{3,2,1,0:T(8,128)S(1)} %bitcast.239, f32[2,4,256,256]{3,2,1,0:T(8,128)S(1)} %collective-permute-done.1), kind=kLoop, calls=%fused_computation.75 | loop fusion | flops 4194304 | bytes 14680064 | tf_op jit(solution)/shard_map/concatenate | solution.py:21
  143.8 45.2 %broadcast_select_fusion = (f32[4,256,256]{2,1,0:T(8,128)}, f32[4,256,256]{2,1,0:T(8,128)S(1)}, f32[4,256,256]{2,1,0:T(8,128)}, f32[4,256,256]{2,1,0:T(8,128)}, f32[4,256,256]{2,1,0:T(8,128)}) fusion(pred[]{:T(512)S(6)} %eq.4, f32[4,256,256]{2,1,0:T(8,128)} %param.8, f32[12,256,256]{2,1,0:T(8,128)} %get-tuple-element.13, f32[2,4,256,256]{3,2,1,0:T(8,128)} %copy-done.1, ...), kind=kLoop, calls=%fused_computation.213 | loop fusion | flops 52690944 | bytes 54525956 | tf_op jit(solution)/shard_map/jit(_where)/select_n | solution.py:26
  189.0 38.8 %all-reduce.10.cloned.1.call-done = f32[4,256,256]{2,1,0:T(8,128)} async-done(((f32[4,256,256]{2,1,0:T(8,128)}), f32[4,256,256]{2,1,0:T(8,128)}) %all-reduce.10.cloned.1.call-update) | async-done | bytes 1048592 | tf_op jit(solution)/shard_map/psum | solution.py:27
  227.8 1.4 pad_maximum_fusion.5
  229.2 3.7 %collective-permute-start.5 = (f32[2,4,256,256]{3,2,1,0:T(8,128)S(1)}, f32[2,4,256,256]{3,2,1,0:T(8,128)S(1)}, u32[]{:S(2)}, u32[]{:S(2)}) collective-permute-start(f32[2,4,256,256]{3,2,1,0:T(8,128)S(1)} %pad_maximum_fusion.5), channel_id=1, source_target_pairs={{0,1},{1,2},{2,3},{3,4},{4,5},{5,6},{6,7},{7,8},{8,9},{9,10},{10,1... | collective-permute-start | bytes 6291464 | tf_op jit(solution)/shard_map/ppermute | solution.py:17
  232.9 2.1 collective-permute-start.4
  235.0 43.3 %collective-permute-done.5 = f32[2,4,256,256]{3,2,1,0:T(8,128)S(1)} collective-permute-done((f32[2,4,256,256]{3,2,1,0:T(8,128)S(1)}, f32[2,4,256,256]{3,2,1,0:T(8,128)S(1)}, u32[]{:S(2)}, u32[]{:S(2)}) %collective-permute-start.5) | collective-permute-done | bytes 2097184 | tf_op jit(solution)/shard_map/ppermute | solution.py:17
  278.3 1.6 collective-permute-done.4
  280.4 3.3 %slice_bitcast_fusion.1 = (f32[12,256,256]{2,1,0:T(8,128)}, f32[12,256,256]{2,1,0:T(8,128)}) fusion(f32[2,12,256,256]{3,2,1,0:T(8,128)S(1)} %pad_maximum_fusion.1), kind=kLoop, calls=%fused_computation.80 | loop fusion | bytes 12582912 | tf_op jit(solution)/shard_map/squeeze | solution.py:91
  283.7 0.9 pad_maximum_fusion.3
  284.9 25.3 %fusion.35 = f32[1,4,256,256]{3,2,1,0:T(8,128)} fusion(f32[4,256,256]{2,1,0:T(8,128)} %get-tuple-element.9, f32[4,256,256]{2,1,0:T(8,128)S(1)} %copy-done.5, f32[4,256,256]{2,1,0:T(8,128)} %param.7, f32[1,4,256,256]{3,2,1,0:T(8,128)S(1)} %copy-done, f32[4,256,256]{2,1,0:T(8,128)} %get-tuple-element.8, f32[4,256,256]{2,1,0:T(8,128)} %get-tuple-element.7, ...), kind=kLoop, calls=%fused_computation.136 | loop fusion | flops 42205184 | bytes 33554436 | tf_op jit(solution)/shard_map/broadcast_in_dim | solution.py:94
  (19 shorter events, 0.9 us)
Async XLA Ops:
  6.5 53.0 %copy-start.4 = (f32[4,256,256]{2,1,0:T(8,128)S(1)}, f32[4,256,256]{2,1,0:T(8,128)}, u32[]{:S(2)}) copy-start(f32[4,256,256]{2,1,0:T(8,128)} %param.8) | copy-start | bytes 3145732
  6.5 44.4 %all-reduce.8.cloned.1.call-start = ((), (), s32[]{:S(2)}) async-start(), calls=%async_computation | async-start | bytes 2097152 | tf_op jit(solution)/shard_map/psum | solution.py:27
  8.9 218.8 %all-reduce.10.cloned.1.call-start = ((), (), s32[]{:S(2)}) async-start(), calls=%async_computation.1 | async-start | bytes 2097152 | tf_op jit(solution)/shard_map/psum | solution.py:27
  53.9 78.8 %collective-permute-start.1 = (f32[2,4,256,256]{3,2,1,0:T(8,128)}, f32[2,4,256,256]{3,2,1,0:T(8,128)S(1)}, u32[]{:S(2)}, u32[]{:S(2)}) collective-permute-start(f32[2,4,256,256]{3,2,1,0:T(8,128)} %pad_maximum_fusion.4), channel_id=1, source_target_pairs={{0,1},{1,2},{2,3},{3,4},{4,5},{5,6},{6,7},{7,8},{8,9},{9,10},{10,1... | collective-permute-start | bytes 6291464 | tf_op jit(solution)/shard_map/ppermute | solution.py:17
  57.6 75.2 %collective-permute-start = (f32[2,4,256,256]{3,2,1,0:T(8,128)}, f32[2,4,256,256]{3,2,1,0:T(8,128)}, u32[]{:S(2)}, u32[]{:S(2)}) collective-permute-start(f32[2,4,256,256]{3,2,1,0:T(8,128)} %pad_maximum_fusion.4), channel_id=1, source_target_pairs={{1,0},{2,1},{3,2},{4,3},{5,4},{6,5},{7,6},{8,7},{9,8},{10,9},{11,1... | collective-permute-start | bytes 6291464 | tf_op jit(solution)/shard_map/ppermute | solution.py:20
  60.6 72.2 %copy-start = (f32[1,4,256,256]{3,2,1,0:T(8,128)S(1)}, f32[1,4,256,256]{3,2,1,0:T(8,128)}, u32[]{:S(2)}) copy-start(f32[1,4,256,256]{3,2,1,0:T(8,128)} %param.6) | copy-start | bytes 3145732
  60.6 65.2 %collective-permute-start.3 = (f32[4,256,256]{2,1,0:T(8,128)}, f32[4,256,256]{2,1,0:T(8,128)}, u32[]{:S(2)}, u32[]{:S(2)}) collective-permute-start(f32[4,256,256]{2,1,0:T(8,128)} %broadcast_add_fusion), channel_id=1, source_target_pairs={{0,1},{1,2},{2,3},{3,4},{4,5},{5,6},{6,7},{7,8},{8,9},{9,10},{10,1... | collective-permute-start | bytes 3145736 | tf_op jit(solution)/shard_map/ppermute | solution.py:17
  64.3 63.1 %collective-permute-start.2 = (f32[4,256,256]{2,1,0:T(8,128)}, f32[4,256,256]{2,1,0:T(8,128)}, u32[]{:S(2)}, u32[]{:S(2)}) collective-permute-start(f32[4,256,256]{2,1,0:T(8,128)} %broadcast_add_fusion), channel_id=1, source_target_pairs={{1,0},{2,1},{3,2},{4,3},{5,4},{6,5},{7,6},{8,7},{9,8},{10,9},{11,1... | collective-permute-start | bytes 3145736 | tf_op jit(solution)/shard_map/ppermute | solution.py:20
  66.3 66.5 %copy-start.2 = (f32[4,256,256]{2,1,0:T(8,128)S(1)}, f32[4,256,256]{2,1,0:T(8,128)}, u32[]{:S(2)}) copy-start(f32[4,256,256]{2,1,0:T(8,128)} %all-reduce.8.cloned.1.call-done) | copy-start | bytes 3145732
  132.8 6.0 %copy-start.1 = (f32[2,4,256,256]{3,2,1,0:T(8,128)}, f32[2,4,256,256]{3,2,1,0:T(8,128)S(1)}, u32[]{:S(2)}) copy-start(f32[2,4,256,256]{3,2,1,0:T(8,128)S(1)} %collective-permute-done.1) | copy-start | bytes 6291460
  227.8 52.2 %copy-start.3 = (f32[4,256,256]{2,1,0:T(8,128)S(1)}, f32[4,256,256]{2,1,0:T(8,128)}, u32[]{:S(2)}) copy-start(f32[4,256,256]{2,1,0:T(8,128)} %all-reduce.10.cloned.1.call-done) | copy-start | bytes 3145732
  229.2 49.1 %collective-permute-start.5 = (f32[2,4,256,256]{3,2,1,0:T(8,128)S(1)}, f32[2,4,256,256]{3,2,1,0:T(8,128)S(1)}, u32[]{:S(2)}, u32[]{:S(2)}) collective-permute-start(f32[2,4,256,256]{3,2,1,0:T(8,128)S(1)} %pad_maximum_fusion.5), channel_id=1, source_target_pairs={{0,1},{1,2},{2,3},{3,4},{4,5},{5,6},{6,7},{7,8},{8,9},{9,10},{10,1... | collective-permute-start | bytes 6291464 | tf_op jit(solution)/shard_map/ppermute | solution.py:17
  232.9 47.0 %collective-permute-start.4 = (f32[2,4,256,256]{3,2,1,0:T(8,128)S(1)}, f32[2,4,256,256]{3,2,1,0:T(8,128)S(1)}, u32[]{:S(2)}, u32[]{:S(2)}) collective-permute-start(f32[2,4,256,256]{3,2,1,0:T(8,128)S(1)} %pad_maximum_fusion.5), channel_id=1, source_target_pairs={{1,0},{2,1},{3,2},{4,3},{5,4},{6,5},{7,6},{8,7},{9,8},{10,9},{11,1... | collective-permute-start | bytes 6291464 | tf_op jit(solution)/shard_map/ppermute | solution.py:20
  283.7 1.2 copy-start.5
Sparse Core Ops, SparseCore 0:
  9.6 41.1 all-reduce.7
  189.1 38.5 all-reduce.9
where the time goes:
time: 317 us
  waiting for transfers between devices  187 us (59%)
  other arithmetic  92.8 us (29%)
  starting transfers between devices  17.1 us (5%)
  between operations  13.5 us (4%)
  local copies, waits for them, and re-layouts  6.93 us (2%)
    ppermute x3, waiting for transfers between devices, with_halo(): lax.ppermute(lax.slice_in_dim(block, block.shape[dim] - width, None, axis...  103 us
    psum x2, waiting for transfers between devices, spread(): return lax.psum(block, axis)  80.7 us
    select_n x2, other arithmetic, spread(): jnp.where(lax.axis_index(axis) == owner, block, jnp.zeros_like(block))  47.6 us
    broadcast_in_dim x1, other arithmetic, on_device(): return now[None]  25.3 us
    concatenate x5, other arithmetic, with_halo(): block = jnp.concatenate([low, block, high], axis=dim)  14.4 us
    ppermute x3, starting transfers between devices, with_halo(): lax.ppermute(lax.slice_in_dim(block, block.shape[dim] - width, None, axis...  11.1 us
    squeeze x2, local copies, waits for them, and re-layouts, on_device(): own_term = operate(both[1])  6.56 us
  transfers between devices with their start and end apart: 8, of which 6 were waited for; matrix products, arithmetic and copies ran while one was open for 2% of the time, Pallas kernels for 0%

commit v1 on v0

--- a/solution.py
+++ b/solution.py
@@ -24,7 +24,7 @@
 
 def spread(block, axis, owner):
     block = jnp.where(lax.axis_index(axis) == owner, block, jnp.zeros_like(block))
-    return lax.psum(block, axis)
+    return lax.all_gather(block, axis).sum(axis=0)
 
 
 def shifted(padded, direction, offset):

time: 317 us -> 302 us (0.953)
  waiting for transfers between devices: 187 us -> 172 us
    psum x2 -> x0, waiting for transfers between devices: 80.7 us -> none  [spread(): return lax.psum(block, axis)]
    all_gather x0 -> x2, waiting for transfers between devices: none -> 66.1 us  [spread(): return lax.all_gather(block, axis).sum(axis=0)]
    reduce_sum x0 -> x2, other arithmetic: none -> 3.71 us  [spread(): return lax.all_gather(block, axis).sum(axis=0)]
where the time goes in v1:
time: 302 us; the launch traced here: 301 us
  waiting for transfers between devices  172 us (57%)
  other arithmetic  91.9 us (30%)
  starting transfers between devices  16.9 us (6%)
  between operations  13.5 us (4%)
  local copies, waits for them, and re-layouts  6.76 us (2%)
    ppermute x3, waiting for transfers between devices, with_halo(): lax.ppermute(lax.slice_in_dim(block, block.shape[dim] - width, None, axis...  103 us
    all_gather x2, waiting for transfers between devices, spread(): return lax.all_gather(block, axis).sum(axis=0)  66.1 us
    select_n x2, other arithmetic, spread(): jnp.where(lax.axis_index(axis) == owner, block, jnp.zeros_like(block))  46.8 us
    broadcast_in_dim x1, other arithmetic, on_device(): return now[None]  24.3 us
    concatenate x5, other arithmetic, with_halo(): block = jnp.concatenate([low, block, high], axis=dim)  14.3 us
    ppermute x3, starting transfers between devices, with_halo(): lax.ppermute(lax.slice_in_dim(block, block.shape[dim] - width, None, axis...  10.9 us
    squeeze x2, local copies, waits for them, and re-layouts, on_device(): own_term = operate(both[1])  6.32 us
  transfers between devices with their start and end apart: 8, of which 6 were waited for; matrix products, arithmetic and copies ran while one was open for 2% of the time, Pallas kernels for 0%

profile of v1, /device:TPU:9, one launch (start us, length us, event | category | flops | bytes accessed | tf_op | source)
XLA Modules:
  0.0 301.4 jit_solution(5975419288900840642)
XLA Ops:
  6.5 2.4 broadcast_select_fusion.1
  9.0 34.2 %all-gather.4.cloned.1.call-done = f32[2,4,256,256]{3,2,1,0:T(8,128)} async-done(((f32[1,4,256,256]{3,2,1,0:T(8,128)}), f32[2,4,256,256]{3,2,1,0:T(8,128)}) %all-gather.4.cloned.1.call-update) | async-done | bytes 2097168 | tf_op jit(solution)/shard_map/all_gather | solution.py:27
  43.2 1.9 reduce_sum.18
  45.1 1.5 pad_maximum_fusion.4
  46.6 3.7 %collective-permute-start.1 = (f32[2,4,256,256]{3,2,1,0:T(8,128)}, f32[2,4,256,256]{3,2,1,0:T(8,128)}, u32[]{:S(2)}, u32[]{:S(2)}) collective-permute-start(f32[2,4,256,256]{3,2,1,0:T(8,128)} %pad_maximum_fusion.4), channel_id=1, source_target_pairs={{0,1},{1,2},{2,3},{3,4},{4,5},{5,6},{6,7},{7,8},{8,9},{9,10},{10,1... | collective-permute-start | bytes 6291464 | tf_op jit(solution)/shard_map/ppermute | solution.py:17
  50.3 1.9 collective-permute-start
  52.2 1.1 broadcast_add_fusion
  53.3 3.6 %collective-permute-start.3 = (f32[4,256,256]{2,1,0:T(8,128)}, f32[4,256,256]{2,1,0:T(8,128)S(1)}, u32[]{:S(2)}, u32[]{:S(2)}) collective-permute-start(f32[4,256,256]{2,1,0:T(8,128)} %broadcast_add_fusion), channel_id=1, source_target_pairs={{0,1},{1,2},{2,3},{3,4},{4,5},{5,6},{6,7},{7,8},{8,9},{9,10},{10,1... | collective-permute-start | bytes 3145736 | tf_op jit(solution)/shard_map/ppermute | solution.py:17
  56.9 1.9 collective-permute-start.2
  58.9 59.6 %collective-permute-done.3 = f32[4,256,256]{2,1,0:T(8,128)S(1)} collective-permute-done((f32[4,256,256]{2,1,0:T(8,128)}, f32[4,256,256]{2,1,0:T(8,128)S(1)}, u32[]{:S(2)}, u32[]{:S(2)}) %collective-permute-start.3) | collective-permute-done | bytes 1048608 | tf_op jit(solution)/shard_map/ppermute | solution.py:17
  118.5 1.6 collective-permute-done.2
  120.1 5.2 %select_maximum_fusion = f32[12,264,264]{2,1,0:T(8,128)} fusion(f32[4,256,256]{2,1,0:T(8,128)} %collective-permute-done.2, f32[4,256,256]{2,1,0:T(8,128)} %broadcast_add_fusion, f32[4,256,256]{2,1,0:T(8,128)S(1)} %collective-permute-done.3), kind=kLoop, calls=%fused_computation.70 | loop fusion | flops 12545280 | bytes 6491136 | tf_op jit(solution)/shard_map/concatenate | solution.py:21
  125.4 2.5 pad_maximum_fusion
  127.9 3.3 %slice_bitcast_fusion.3 = (f32[12,256,256]{2,1,0:T(8,128)}, f32[12,256,256]{2,1,0:T(8,128)}) fusion(f32[2,12,256,256]{3,2,1,0:T(8,128)S(1)} %pad_maximum_fusion), kind=kLoop, calls=%fused_computation.82 | loop fusion | bytes 12582912 | tf_op jit(solution)/shard_map/squeeze | solution.py:91
  131.1 5.2 %pad_maximum_fusion.2 = (f32[2,8,256,256]{3,2,1,0:T(8,128)}, f32[2,8,256,256]{3,2,1,0:T(8,128)}) fusion(f32[2,4,256,256]{3,2,1,0:T(8,128)} %collective-permute-done, f32[1,4,256,256]{3,2,1,0:T(8,128)S(1)} %copy-done, f32[1,4,256,256]{3,2,1,0:T(8,128)S(1)} %bitcast.239, f32[2,4,256,256]{3,2,1,0:T(8,128)} %collective-permute-done.1), kind=kLoop, calls=%fused_computation.75 | loop fusion | flops 4194304 | bytes 14680064 | tf_op jit(solution)/shard_map/concatenate | solution.py:21
  136.4 44.4 %broadcast_select_fusion = (f32[4,256,256]{2,1,0:T(8,128)}, f32[4,256,256]{2,1,0:T(8,128)S(1)}, f32[4,256,256]{2,1,0:T(8,128)}, f32[4,256,256]{2,1,0:T(8,128)}, f32[4,256,256]{2,1,0:T(8,128)}) fusion(pred[]{:T(512)S(6)} %eq.4, f32[4,256,256]{2,1,0:T(8,128)} %param.8, f32[12,256,256]{2,1,0:T(8,128)} %get-tuple-element.13, ...), kind=kLoop, calls=%fused_computation.211 | loop fusion | flops 52690944 | bytes 54525956 | tf_op jit(solution)/shard_map/jit(_where)/select_n | solution.py:26
  180.9 31.8 %all-gather.6.cloned.1.call-done = f32[8,256,256]{2,1,0:T(8,128)} async-done(((f32[4,256,256]{2,1,0:T(8,128)}), f32[8,256,256]{2,1,0:T(8,128)}) %all-gather.6.cloned.1.call-update) | async-done | bytes 2097168 | tf_op jit(solution)/shard_map/all_gather | solution.py:27
  212.7 1.9 reduce_sum.19
  214.7 3.7 %collective-permute-start.5 = (f32[2,4,256,256]{3,2,1,0:T(8,128)S(1)}, f32[2,4,256,256]{3,2,1,0:T(8,128)S(1)}, u32[]{:S(2)}, u32[]{:S(2)}) collective-permute-start(f32[2,4,256,256]{3,2,1,0:T(8,128)S(1)} %pad_maximum_fusion.5), channel_id=1, source_target_pairs={{0,1},{1,2},{2,3},{3,4},{4,5},{5,6},{6,7},{7,8},{8,9},{9,10},{10,1... | collective-permute-start | bytes 6291464 | tf_op jit(solution)/shard_map/ppermute | solution.py:17
  218.4 2.1 collective-permute-start.4
  220.5 43.3 %collective-permute-done.5 = f32[2,4,256,256]{3,2,1,0:T(8,128)S(1)} collective-permute-done((f32[2,4,256,256]{3,2,1,0:T(8,128)S(1)}, f32[2,4,256,256]{3,2,1,0:T(8,128)S(1)}, u32[]{:S(2)}, u32[]{:S(2)}) %collective-permute-start.5) | collective-permute-done | bytes 2097184 | tf_op jit(solution)/shard_map/ppermute | solution.py:17
  263.8 1.6 collective-permute-done.4
  266.0 3.1 %slice_bitcast_fusion.1 = (f32[12,256,256]{2,1,0:T(8,128)}, f32[12,256,256]{2,1,0:T(8,128)}) fusion(f32[2,12,256,256]{3,2,1,0:T(8,128)S(1)} %pad_maximum_fusion.1), kind=kLoop, calls=%fused_computation.80 | loop fusion | bytes 12582912 | tf_op jit(solution)/shard_map/squeeze | solution.py:91
  270.3 24.3 %fusion.35 = f32[1,4,256,256]{3,2,1,0:T(8,128)} fusion(f32[4,256,256]{2,1,0:T(8,128)} %get-tuple-element.9, f32[4,256,256]{2,1,0:T(8,128)S(1)} %copy-done.2, f32[4,256,256]{2,1,0:T(8,128)} %param.7, f32[1,4,256,256]{3,2,1,0:T(8,128)S(1)} %copy-done, f32[4,256,256]{2,1,0:T(8,128)} %get-tuple-element.8, f32[4,256,256]{2,1,0:T(8,128)} %get-tuple-element.7, ...), kind=kLoop, calls=%fused_computation.136 | loop fusion | flops 42205184 | bytes 33554436 | tf_op jit(solution)/shard_map/broadcast_in_dim | solution.py:94
  (17 shorter events, 2.0 us)
Async XLA Ops:
  6.5 38.5 %copy-start = (f32[1,4,256,256]{3,2,1,0:T(8,128)S(1)}, f32[1,4,256,256]{3,2,1,0:T(8,128)}, u32[]{:S(2)}) copy-start(f32[1,4,256,256]{3,2,1,0:T(8,128)} %param.6) | copy-start | bytes 3145732
  6.5 36.7 %all-gather.4.cloned.1.call-start = ((), (), s32[]{:S(2)}) async-start(), calls=%async_computation | async-start | bytes 3145728 | tf_op jit(solution)/shard_map/all_gather | solution.py:27
  8.9 43.3 %copy-start.1 = (f32[4,256,256]{2,1,0:T(8,128)S(1)}, f32[4,256,256]{2,1,0:T(8,128)}, u32[]{:S(2)}) copy-start(f32[4,256,256]{2,1,0:T(8,128)} %param.8) | copy-start | bytes 3145732
  8.9 203.8 %all-gather.6.cloned.1.call-start = ((), (), s32[]{:S(2)}) async-start(), calls=%async_computation.1 | async-start | bytes 3145728 | tf_op jit(solution)/shard_map/all_gather | solution.py:27
  46.6 78.7 %collective-permute-start.1 = (f32[2,4,256,256]{3,2,1,0:T(8,128)}, f32[2,4,256,256]{3,2,1,0:T(8,128)}, u32[]{:S(2)}, u32[]{:S(2)}) collective-permute-start(f32[2,4,256,256]{3,2,1,0:T(8,128)} %pad_maximum_fusion.4), channel_id=1, source_target_pairs={{0,1},{1,2},{2,3},{3,4},{4,5},{5,6},{6,7},{7,8},{8,9},{9,10},{10,1... | collective-permute-start | bytes 6291464 | tf_op jit(solution)/shard_map/ppermute | solution.py:17
  50.3 75.1 %collective-permute-start = (f32[2,4,256,256]{3,2,1,0:T(8,128)}, f32[2,4,256,256]{3,2,1,0:T(8,128)}, u32[]{:S(2)}, u32[]{:S(2)}) collective-permute-start(f32[2,4,256,256]{3,2,1,0:T(8,128)} %pad_maximum_fusion.4), channel_id=1, source_target_pairs={{1,0},{2,1},{3,2},{4,3},{5,4},{6,5},{7,6},{8,7},{9,8},{10,9},{11,1... | collective-permute-start | bytes 6291464 | tf_op jit(solution)/shard_map/ppermute | solution.py:20
  53.3 65.2 %collective-permute-start.3 = (f32[4,256,256]{2,1,0:T(8,128)}, f32[4,256,256]{2,1,0:T(8,128)S(1)}, u32[]{:S(2)}, u32[]{:S(2)}) collective-permute-start(f32[4,256,256]{2,1,0:T(8,128)} %broadcast_add_fusion), channel_id=1, source_target_pairs={{0,1},{1,2},{2,3},{3,4},{4,5},{5,6},{6,7},{7,8},{8,9},{9,10},{10,1... | collective-permute-start | bytes 3145736 | tf_op jit(solution)/shard_map/ppermute | solution.py:17
  56.9 63.2 %collective-permute-start.2 = (f32[4,256,256]{2,1,0:T(8,128)}, f32[4,256,256]{2,1,0:T(8,128)}, u32[]{:S(2)}, u32[]{:S(2)}) collective-permute-start(f32[4,256,256]{2,1,0:T(8,128)} %broadcast_add_fusion), channel_id=1, source_target_pairs={{1,0},{2,1},{3,2},{4,3},{5,4},{6,5},{7,6},{8,7},{9,8},{10,9},{11,1... | collective-permute-start | bytes 3145736 | tf_op jit(solution)/shard_map/ppermute | solution.py:20
  118.5 9.4 %copy-start.3 = (f32[4,256,256]{2,1,0:T(8,128)}, f32[4,256,256]{2,1,0:T(8,128)S(1)}, u32[]{:S(2)}) copy-start(f32[4,256,256]{2,1,0:T(8,128)S(1)} %collective-permute-done.3) | copy-start | bytes 3145732
  214.7 49.1 %collective-permute-start.5 = (f32[2,4,256,256]{3,2,1,0:T(8,128)S(1)}, f32[2,4,256,256]{3,2,1,0:T(8,128)S(1)}, u32[]{:S(2)}, u32[]{:S(2)}) collective-permute-start(f32[2,4,256,256]{3,2,1,0:T(8,128)S(1)} %pad_maximum_fusion.5), channel_id=1, source_target_pairs={{0,1},{1,2},{2,3},{3,4},{4,5},{5,6},{6,7},{7,8},{8,9},{9,10},{10,1... | collective-permute-start | bytes 6291464 | tf_op jit(solution)/shard_map/ppermute | solution.py:17
  218.4 47.0 %collective-permute-start.4 = (f32[2,4,256,256]{3,2,1,0:T(8,128)S(1)}, f32[2,4,256,256]{3,2,1,0:T(8,128)S(1)}, u32[]{:S(2)}, u32[]{:S(2)}) collective-permute-start(f32[2,4,256,256]{3,2,1,0:T(8,128)S(1)} %pad_maximum_fusion.5), channel_id=1, source_target_pairs={{1,0},{2,1},{3,2},{4,3},{5,4},{6,5},{7,6},{8,7},{9,8},{10,9},{11,1... | collective-permute-start | bytes 6291464 | tf_op jit(solution)/shard_map/ppermute | solution.py:20
  269.1 1.2 copy-start.2
Sparse Core Ops, SparseCore 0:
  9.1 34.1 all-gather.3
  181.0 31.6 all-gather.5
